TPU v7x, 256 devices: a whole 4x4x8 slice. The times are simulated.
256 devices in a mesh: tok: 8 (over z), tp: 16 (over y, x), grp: 2 (over core).
Axes of the slice: x: 4, y: 4, z: 8, core: 2. Of those that a mesh axis runs over, the one named last changes fastest.
Arguments:
- hidden: bfloat16 [2048, 6144], P(('tok', 'grp'), 'tp'), may hold values from -6 to 6
- gain: bfloat16 [6144], P('tp'), may hold values from 0.5 to 1.5
- expert_ids: int32 [2048, 2], P(('tok', 'grp')), may hold values from 0 to 7, all different within a row; in each aligned block of 128 rows (0 to 127, 128 to 255, ...) at most 40 rows name the same one
- gate_weights: float32 [2048, 2], P(('tok', 'grp')), may hold values from 0.1 to 0.9
- segment_ids: int32 [2048], P(('tok', 'grp')), may hold values from 0 to 15, never falling along the last dimension, each value on 1 to 384 neighbouring positions
- upstream: bfloat16 [2048, 6144], P(('tok', 'grp'), 'tp'), may hold values from -6 to 6
- w_gate: bfloat16 [8, 6144, 8192], P('tok', None, ('tp', 'grp')), may hold values from -0.078125 to 0.078125
- w_up: bfloat16 [8, 6144, 8192], P('tok', None, ('tp', 'grp')), may hold values from -0.078125 to 0.078125
- w_down: bfloat16 [8, 8192, 6144], P('tok', ('tp', 'grp')), may hold values from -0.0625 to 0.0625
Outputs:
- mixed: bfloat16 [2048, 6144], P(('tok', 'grp'), 'tp')
- importance: float32 [8, 8192], P('tok', ('tp', 'grp'))
Inputs may be any that keep to these rules, and one draw needn't show every extreme that they name: `expert_ids`: each token names 2 different experts. Within the tokens of one token shard (aligned blocks of 128 rows) no expert is named by more than 40 tokens, and in some block one expert is named by exactly 40. `segment_ids`: never falling along the tokens; every document holds between 1 and 384 tokens.
All inputs are finite; a program needn't handle non-finite values.
Results may differ from a plain program's by a relative error of at most 0.0095.
Values may be sent and summed in bfloat16 or wider, within the bound.
No kernel may reach another device: no remote copies, remote signals or barrier semaphores. Data moves between devices by JAX's collectives and lax.ppermute only.
A program may use at most 128 MiB of HBM per device.

v0:
```python
import jax
import jax.numpy as jnp
from jax import lax
from jax.sharding import PartitionSpec as P


def expert_pass(rows_in, cot_in, gate_mat, up_mat, down_mat):
    gate_pre = jnp.dot(rows_in, gate_mat, preferred_element_type=jnp.float32)
    up_proj = jnp.dot(rows_in, up_mat, preferred_element_type=jnp.float32)
    sigmoid_gate = jax.nn.sigmoid(gate_pre)
    activated = gate_pre * sigmoid_gate
    hidden_act = (activated * up_proj).astype(jnp.bfloat16)
    grad_act = lax.dot_general(
        cot_in, down_mat, (((1,), (1,)), ((), ())), preferred_element_type=jnp.float32
    )
    grad_gate = (
        grad_act * up_proj * sigmoid_gate * (1.0 + gate_pre * (1.0 - sigmoid_gate))
    ).astype(jnp.bfloat16)
    grad_up = (grad_act * activated).astype(jnp.bfloat16)
    grad_wgate = lax.dot_general(
        rows_in, grad_gate, (((0,), (0,)), ((), ())), preferred_element_type=jnp.float32
    )
    grad_wup = lax.dot_general(
        rows_in, grad_up, (((0,), (0,)), ((), ())), preferred_element_type=jnp.float32
    )
    grad_wdown = lax.dot_general(
        hidden_act, cot_in, (((0,), (0,)), ((), ())), preferred_element_type=jnp.float32
    )
    scores = jnp.sum(jnp.abs(grad_wgate * gate_mat.astype(jnp.float32)), axis=0)
    scores = scores + jnp.sum(jnp.abs(grad_wup * up_mat.astype(jnp.float32)), axis=0)
    scores = scores + jnp.sum(jnp.abs(grad_wdown * down_mat.astype(jnp.float32)), axis=1)
    return (hidden_act, scores)


def on_device(hidden, gain, expert_ids, gate_weights, segment_ids, upstream, w_gate, w_up, w_down):
    rows_here = hidden.shape[0]
    top_count = expert_ids.shape[1]
    experts = lax.axis_size("tok")
    groups = lax.axis_size("grp")
    capacity = 5 * rows_here // (2 * experts)
    width = w_gate.shape[1]
    documents = jnp.arange(experts * groups, dtype=jnp.int32)
    doc_onehot = (segment_ids[:, None] == documents[None, :]).astype(jnp.float32)
    doc_len = lax.psum(jnp.sum(doc_onehot, axis=0), ("tok", "grp"))
    tok_len = jnp.sum(doc_onehot * doc_len[None, :], axis=1)
    tok_weight = rows_here / tok_len
    onehot = (
        expert_ids.reshape(-1)[:, None] == jnp.arange(experts, dtype=jnp.int32)[None, :]
    ).astype(jnp.int32)
    before = jnp.cumsum(onehot, axis=0) - onehot
    slot_ids = jnp.sum(before * onehot, axis=1).reshape(rows_here, top_count)
    targets = expert_ids * capacity + slot_ids
    all_slots = jnp.arange(experts * capacity, dtype=jnp.int32)
    matches = all_slots[:, None, None] == targets[None, :, :]
    placing = jnp.any(matches, axis=2).astype(jnp.bfloat16)
    scaled = gate_weights * tok_weight[:, None]
    slot_scale = jnp.sum(jnp.where(matches, scaled[None, :, :], 0.0), axis=(1, 2))
    combining = jnp.sum(jnp.where(matches, gate_weights[None, :, :], 0.0), axis=2)
    wide_hidden = hidden.astype(jnp.float32)
    squares = lax.psum(jnp.sum(wide_hidden * wide_hidden, axis=1), "tp")
    scaling = lax.rsqrt(squares / width + 1e-05)
    normed = (wide_hidden * scaling[:, None] * gain.astype(jnp.float32)[None, :]).astype(
        jnp.bfloat16
    )
    block_rows = jnp.dot(placing, normed, preferred_element_type=jnp.float32).astype(jnp.bfloat16)
    block_cot = jnp.dot(placing, upstream, preferred_element_type=jnp.float32) * slot_scale[:, None]
    block_rows = block_rows.reshape(experts, capacity, -1)
    block_cot = block_cot.astype(jnp.bfloat16).reshape(experts, capacity, -1)
    came_rows, came_cot = (
        lax.all_to_all(block_rows, "tok", split_axis=0, concat_axis=0, tiled=True),
        lax.all_to_all(block_cot, "tok", split_axis=0, concat_axis=0, tiled=True),
    )
    part_rows, part_cot = (
        lax.all_gather(came_rows, "tp", axis=2, tiled=True),
        lax.all_gather(came_cot, "tp", axis=2, tiled=True),
    )
    pooled_rows, pooled_cot = (
        lax.all_gather(part_rows, "grp", axis=0, tiled=True),
        lax.all_gather(part_cot, "grp", axis=0, tiled=True),
    )
    rows_in = pooled_rows.reshape(-1, width)
    cot_in = pooled_cot.reshape(-1, width)
    gate_mat = w_gate[0]
    up_mat = w_up[0]
    down_mat = w_down[0]
    hidden_act, scores = expert_pass(rows_in, cot_in, gate_mat, up_mat, down_mat)
    importance = scores / (rows_here * experts * groups)
    partial_value = lax.psum_scatter(
        lax.dot_general(
            down_mat, hidden_act, (((0,), (1,)), ((), ())), preferred_element_type=jnp.float32
        ).astype(jnp.bfloat16),
        "tp",
        scatter_dimension=0,
        tiled=True,
    )
    summed = lax.psum_scatter(partial_value, "grp", scatter_dimension=1, tiled=True).astype(
        jnp.float32
    )
    slice_width = summed.shape[0]
    outgoing = summed.astype(jnp.bfloat16).reshape(slice_width, experts, capacity)
    returned = lax.all_to_all(outgoing, "tok", split_axis=1, concat_axis=1, tiled=True)
    returned = returned.reshape(slice_width, experts * capacity).astype(jnp.float32)
    combined = lax.dot_general(
        combining,
        returned,
        (((0,), (1,)), ((), ())),
        precision=lax.Precision.HIGHEST,
        preferred_element_type=jnp.float32,
    )
    mixed = (hidden.astype(jnp.float32) + combined).astype(jnp.bfloat16)
    return (mixed, importance[None, :])


def solution(mesh):
    placed = (
        P(("tok", "grp"), "tp"),
        P("tp"),
        P(("tok", "grp"), None),
        P(("tok", "grp"), None),
        P(("tok", "grp")),
        P(("tok", "grp"), "tp"),
        P("tok", None, ("tp", "grp")),
        P("tok", None, ("tp", "grp")),
        P("tok", ("tp", "grp"), None),
    )
    return jax.shard_map(
        on_device,
        mesh=mesh,
        in_specs=placed,
        out_specs=(P(("tok", "grp"), "tp"), P("tok", ("tp", "grp"))),
        check_vma=False,
    )
```

profile of v0, /device:TPU:1, one launch (start us, length us, event | category | flops | bytes accessed | tf_op | source)
XLA Modules:
  0.0 378.7 jit_solution(2218602018310981666)
XLA Ops:
  7.2 0.9 copy.31
  8.2 0.1 eq.56
  8.3 0.1 eq.52
  8.5 1.0 fusion.19
  9.5 34.2 %psum.14 = f32[128]{0:T(128)S(1)} all-reduce(f32[128]{0:T(128)S(1)} %fusion.19), channel_id=1, replica_groups=mesh['tok'=8,'tp'=16,'grp'=2] {'tp'}, use_global_device_ids=true, to_apply=%region_6.7 | all-reduce | flops 128 | bytes 1024 | tf_op jit(solution)/shard_map/psum | solution.py:60
  43.7 0.7 convert_element_type.60
  44.4 0.6 reduce-window.6
  45.0 0.2 slice_reduce_fusion
  45.2 0.1 fusion.27
  45.3 0.1 reshape.79
  45.5 0.1 copy.33
  45.5 0.7 multiply_add_fusion
  46.3 1.2 convolution_convert_fusion.1
  47.5 17.2 %all_to_all.15 = bf16[8,40,384]{2,1,0:T(8,128)(2,1)} all-to-all(bf16[8,40,384]{2,1,0:T(8,128)(2,1)S(1)} %bitcast.56), channel_id=1, replica_groups=mesh['tok'=8,'tp'=16,'grp'=2] {'tok'}, dimensions={0} | all-to-all | bytes 491520 | tf_op jit(solution)/shard_map/all_to_all | solution.py:70
  64.7 0.0 all-gather.9.cloned.1.call-start
  64.8 0.8 convert_reduce_fusion
  65.6 32.2 %psum.15 = f32[16]{0:T(128)S(1)} all-reduce(f32[16]{0:T(128)S(1)} %convert_reduce_fusion), channel_id=1, replica_groups=mesh['tok'=8,'tp'=16,'grp'=2] {'tok','grp'}, use_global_device_ids=true, to_apply=%region_10.11 | all-reduce | flops 16 | bytes 128 | tf_op jit(solution)/shard_map/psum | solution.py:44
  97.8 0.7 select_reduce_fusion.2
  98.5 0.7 broadcast_multiply_fusion
  99.2 1.5 select_reduce_fusion
  100.7 0.2 fusion.14
  101.0 12.8 %all_to_all.16 = bf16[8,40,384]{2,1,0:T(8,128)(2,1)} all-to-all(bf16[8,40,384]{2,1,0:T(8,128)(2,1)S(1)} %bitcast.57), channel_id=1, replica_groups=mesh['tok'=8,'tp'=16,'grp'=2] {'tok'}, dimensions={0} | all-to-all | bytes 491520 | tf_op jit(solution)/shard_map/all_to_all | solution.py:71
  113.8 0.0 all-gather.7.cloned.1.call-start
  113.8 10.2 %all-gather.5.cloned.1.call-done = bf16[8,40,6144]{2,1,0:T(8,128)(2,1)} async-done(((bf16[8,40,384]{2,1,0:T(8,128)(2,1)}), bf16[8,40,6144]{2,1,0:T(8,128)(2,1)}) %all-gather.5.cloned.1.call-update) | async-done | bytes 3932176 | tf_op jit(solution)/shard_map/all_gather | solution.py:74
  124.1 0.0 all-gather.11.cloned.1.call-start
  124.1 62.4 %all-gather.9.cloned.1.call-done = bf16[8,40,6144]{2,1,0:T(8,128)(2,1)} async-done(((bf16[8,40,384]{2,1,0:T(8,128)(2,1)}), bf16[8,40,6144]{2,1,0:T(8,128)(2,1)}) %all-gather.9.cloned.1.call-update) | async-done | bytes 3932176 | tf_op jit(solution)/shard_map/all_gather | solution.py:75
  186.5 0.0 reduce-scatter.7.cloned.1.call-start
  186.5 27.7 %all-gather.7.cloned.1.call-done = bf16[16,40,6144]{2,1,0:T(8,128)(2,1)} async-done(((bf16[8,40,6144]{2,1,0:T(8,128)(2,1)}), bf16[16,40,6144]{2,1,0:T(8,128)(2,1)}) %all-gather.7.cloned.1.call-update) | async-done | bytes 7864336 | tf_op jit(solution)/shard_map/all_gather | solution.py:78
  214.2 5.6 %fusion.9 = f32[640,256]{1,0:T(8,128)S(1)} fusion(bf16[640,6144]{1,0:T(8,128)(2,1)} %bitcast.60, bf16[1,6144,256]{2,1,0:T(8,128)(2,1)S(1)} %copy-done.4), kind=kOutput, calls=%fused_computation.13 | convolution fusion | flops 2013265920 | bytes 11665408 | tf_op jit(solution)/shard_map/dot_general | solution.py:8
  219.8 0.8 copy-done.6
  220.6 3.0 multiply_convert_fusion.2
  223.6 0.7 copy-done.2
  224.4 6.1 %fusion = bf16[6144,640]{0,1:T(8,128)(2,1)} fusion(bf16[640,256]{1,0:T(8,128)(2,1)S(1)} %get-tuple-element.4, bf16[1,256,6144]{2,1,0:T(8,128)(2,1)S(1)} %copy-done.1), kind=kOutput, calls=%fused_computation.1 | convolution fusion | flops 2017198080 | bytes 11337728 | tf_op jit(solution)/shard_map/dot_general | solution.py:89
  230.5 10.7 %copy.34 = bf16[6144,640]{1,0:T(8,128)(2,1)} copy(bf16[6144,640]{0,1:T(8,128)(2,1)} %fusion) | data formatting | bytes 15728640
  241.2 0.2 reduce-scatter.5.cloned.1.call-start
  241.5 0.1 all-gather.11.cloned.1.call-done
  241.6 5.6 %fusion.4 = f32[640,256]{1,0:T(8,128)S(1)} fusion(bf16[640,6144]{1,0:T(8,128)(2,1)} %bitcast.53, bf16[1,256,6144]{2,1,0:T(8,128)(2,1)S(1)} %copy-done.1), kind=kOutput, calls=%fused_computation.8 | convolution fusion | flops 2013265920 | bytes 11665408 | tf_op jit(solution)/shard_map/dot_general | solution.py:13
  247.2 0.8 copy-done.9
  248.1 6.2 %fusion.11 = f32[256]{0:T(256)S(1)} fusion(bf16[1,6144,256]{2,1,0:T(8,128)(2,1)S(1)} %copy-done.5, bf16[640,6144]{1,0:T(8,128)(2,1)} %bitcast.61, f32[640,256]{1,0:T(8,128)S(1)} %copy-done.8, f32[640,256]{1,0:T(8,128)S(1)} %fusion.4, f32[640,256]{1,0:T(8,128)S(1)} %copy-done.10), kind=kOutput, calls=%fused_computation.15 | convolution fusion | flops 2021195520 | bytes 12977152 | tf_op jit(solution)/shard_map/dot_general | solution.py:20
  254.3 80.1 %reduce-scatter.7.cloned.1.call-done = bf16[384,640]{1,0:T(8,128)(2,1)} async-done(((bf16[6144,640]{1,0:T(8,128)(2,1)}), bf16[384,640]{1,0:T(8,128)(2,1)}) %reduce-scatter.7.cloned.1.call-update) | async-done | bytes 491536
  334.4 2.0 copy.35
  336.5 7.4 %fusion.12 = f32[256]{0:T(256)S(1)} fusion(bf16[1,6144,256]{2,1,0:T(8,128)(2,1)} %param.16, bf16[640,6144]{1,0:T(8,128)(2,1)} %bitcast.62, f32[640,256]{1,0:T(8,128)} %copy-done.9, f32[640,256]{1,0:T(8,128)} %copy-done.7), kind=kOutput, calls=%fused_computation.16 | convolution fusion | flops 2020540160 | bytes 12321792 | tf_op jit(solution)/shard_map/dot_general | solution.py:23
  343.8 7.7 %reduce-scatter.5.cloned.1.call-done = bf16[384,320]{0,1:T(8,128)(2,1)} async-done(((bf16[384,640]{0,1:T(8,128)(2,1)}), bf16[384,320]{0,1:T(8,128)(2,1)}) %reduce-scatter.5.cloned.1.call-update) | async-done | bytes 245776 | tf_op jit(solution)/shard_map/reduce_scatter | solution.py:96
  351.5 6.5 %all-to-all-start.1 = ((bf16[384,8,40]{0,2,1:T(8,128)(2,1)}), bf16[384,8,40]{0,2,1:T(8,128)(2,1)S(1)}, u32[]{:S(2)}, u32[]{:S(2)}) async-start(bf16[384,8,40]{0,2,1:T(8,128)(2,1)} %bitcast.58), calls=%async_computation.2 | async-start | bytes 491520 | tf_op jit(solution)/shard_map/all_to_all | solution.py:101
  358.0 6.5 %fusion.13 = f32[256]{0:T(256)S(1)} fusion(bf16[1,256,6144]{2,1,0:T(8,128)(2,1)S(1)} %copy-done.1, bf16[640,256]{1,0:T(8,128)(2,1)} %copy-done.2, bf16[640,6144]{1,0:T(8,128)(2,1)} %bitcast.54), kind=kOutput, calls=%fused_computation.17 | convolution fusion | flops 2019557120 | bytes 11338752 | tf_op jit(solution)/shard_map/dot_general | solution.py:26
  364.5 0.6 add_multiply_fusion
  365.0 4.8 %all-to-all-done.1 = bf16[384,8,40]{0,2,1:T(8,128)(2,1)S(1)} async-done(((bf16[384,8,40]{0,2,1:T(8,128)(2,1)}), bf16[384,8,40]{0,2,1:T(8,128)(2,1)S(1)}, u32[]{:S(2)}, u32[]{:S(2)}) %all-to-all-start.1) | async-done | bytes 245792 | tf_op jit(solution)/shard_map/all_to_all | solution.py:101
  369.8 2.0 fusion.15
  (32 shorter events, 0.3 us)
Async XLA Ops:
  7.2 93.6 %copy-start = (bf16[128,384]{1,0:T(8,128)(2,1)S(1)}, bf16[128,384]{1,0:T(8,128)(2,1)}, u32[]{:S(2)}) copy-start(bf16[128,384]{1,0:T(8,128)(2,1)} %param.14) | copy-start | bytes 294916
  7.2 207.0 %copy-start.4 = (bf16[1,6144,256]{2,1,0:T(8,128)(2,1)S(1)}, bf16[1,6144,256]{2,1,0:T(8,128)(2,1)}, u32[]{:S(2)}) copy-start(bf16[1,6144,256]{2,1,0:T(8,128)(2,1)} %param.15) | copy-start | bytes 9437188
  7.2 116.8 %all-gather.5.cloned.1.call-start = ((), (), s32[]{:S(2)}) async-start(), calls=%async_computation.5 | async-start | bytes 4177920 | tf_op jit(solution)/shard_map/all_gather | solution.py:74
  64.7 121.7 %all-gather.9.cloned.1.call-start = ((), (), s32[]{:S(2)}) async-start(), calls=%async_computation.8 | async-start | bytes 4177920 | tf_op jit(solution)/shard_map/all_gather | solution.py:75
  113.8 100.4 %all-gather.7.cloned.1.call-start = ((), (), s32[]{:S(2)}) async-start(), calls=%async_computation.6 | async-start | bytes 11796480 | tf_op jit(solution)/shard_map/all_gather | solution.py:78
  124.1 117.6 %all-gather.11.cloned.1.call-start = ((), (), s32[]{:S(2)}) async-start(), calls=%async_computation.9 | async-start | bytes 11796480 | tf_op jit(solution)/shard_map/all_gather | solution.py:79
  186.5 147.9 %reduce-scatter.7.cloned.1.call-start = ((), (), s32[]{:S(2)}) async-start(), calls=%async_computation.10 | async-start | bytes 8355840
  214.2 5.6 %copy-start.3 = (bf16[16,40,6144]{2,1,0:T(8,128)(2,1)S(1)}, bf16[16,40,6144]{2,1,0:T(8,128)(2,1)}, u32[]{:S(2)}) copy-start(bf16[16,40,6144]{2,1,0:T(8,128)(2,1)} %all-gather.7.cloned.1.call-done) | copy-start | bytes 23592964
  214.2 6.4 %copy-start.6 = (bf16[1,6144,256]{2,1,0:T(8,128)(2,1)S(1)}, bf16[1,6144,256]{2,1,0:T(8,128)(2,1)}, u32[]{:S(2)}) copy-start(bf16[1,6144,256]{2,1,0:T(8,128)(2,1)} %param.16) | copy-start | bytes 9437188
  220.6 3.0 copy-start.7
  220.6 3.8 copy-start.1
  223.6 0.7 copy-start.2
  241.2 110.2 %reduce-scatter.5.cloned.1.call-start = ((), (), s32[]{:S(2)}) async-start(), calls=%async_computation.7 | async-start | bytes 737280 | tf_op jit(solution)/shard_map/reduce_scatter | solution.py:96
  241.6 6.5 %copy-start.5 = (bf16[1,6144,256]{2,1,0:T(8,128)(2,1)S(1)}, bf16[1,6144,256]{2,1,0:T(8,128)(2,1)}, u32[]{:S(2)}) copy-start(bf16[1,6144,256]{2,1,0:T(8,128)(2,1)} %param.15) | copy-start | bytes 9437188
  241.6 6.5 %copy-start.8 = (f32[640,256]{1,0:T(8,128)S(1)}, f32[640,256]{1,0:T(8,128)}, u32[]{:S(2)}) copy-start(f32[640,256]{1,0:T(8,128)} %copy-done.7) | copy-start | bytes 1966084
  241.6 6.5 %copy-start.10 = (f32[640,256]{1,0:T(8,128)S(1)}, f32[640,256]{1,0:T(8,128)}, u32[]{:S(2)}) copy-start(f32[640,256]{1,0:T(8,128)} %get-tuple-element.5) | copy-start | bytes 1966084
  247.2 0.8 copy-start.9
  351.5 18.3 %all-to-all-start.1 = ((bf16[384,8,40]{0,2,1:T(8,128)(2,1)}), bf16[384,8,40]{0,2,1:T(8,128)(2,1)S(1)}, u32[]{:S(2)}, u32[]{:S(2)}) async-start(bf16[384,8,40]{0,2,1:T(8,128)(2,1)} %bitcast.58), calls=%async_computation.2 | async-start | bytes 491520 | tf_op jit(solution)/shard_map/all_to_all | solution.py:101
Sparse Core Ops, SparseCore 0:
  64.9 59.1 all-gather.4
  126.4 59.9 all-gather.8
  188.3 25.9 all-gather.6
  215.9 25.6 all-gather.10
  245.3 89.1 reduce-scatter.6
  336.8 14.6 reduce-scatter.4
where the time goes:
time: 379 us
  waiting for transfers between devices  193 us (51%)
  blocking collectives  96.5 us (25%)
  matrix products  43.9 us (12%)
  local copies, waits for them, and re-layouts  16.8 us (4%)
  between operations  14.2 us (4%)
  other arithmetic  7.42 us (2%)
  starting transfers between devices  6.89 us (2%)
    unnamed x7, waiting for transfers between devices  80.2 us
    all_gather x1, waiting for transfers between devices, on_device(): lax.all_gather(came_cot, 'tp', axis=2, tiled=True)  62.4 us
    psum x1, blocking collectives, on_device(): squares = lax.psum(jnp.sum(wide_hidden * wide_hidden, axis=1), 'tp')  34.2 us
    psum x1, blocking collectives, on_device(): doc_len = lax.psum(jnp.sum(doc_onehot, axis=0), ('tok', 'grp'))  32.2 us
    all_gather x1, waiting for transfers between devices, on_device(): lax.all_gather(part_rows, 'grp', axis=0, tiled=True)  27.7 us
    all_to_all x1, blocking collectives, on_device(): lax.all_to_all(block_rows, 'tok', split_axis=0, concat_axis=0, tiled=True)  17.2 us
    unnamed x25, local copies, waits for them, and re-layouts  16.1 us
    all_to_all x1, blocking collectives, on_device(): lax.all_to_all(block_cot, 'tok', split_axis=0, concat_axis=0, tiled=True)  12.8 us
  transfers between devices with their start and end apart: 7, of which 7 were waited for; matrix products, arithmetic and copies ran while one was open for 15% of the time, Pallas kernels for 0%

commit v1 on v0

--- a/solution.py
+++ b/solution.py
@@ -75,7 +75,9 @@
         lax.all_gather(came_cot, "tp", axis=2, tiled=True),
     )
     pooled_rows, pooled_cot = (
-        lax.all_gather(part_rows, "grp", axis=0, tiled=True),
+        jnp.concatenate(
+            lax.all_to_all(jnp.stack([part_rows] * lax.axis_size("grp")), "grp", 0, 0), axis=0
+        ),
         lax.all_gather(part_cot, "grp", axis=0, tiled=True),
     )
     rows_in = pooled_rows.reshape(-1, width)

time: 379 us -> 349 us (0.921)
  waiting for transfers between devices: 193 us -> 158 us
  matrix products: 43.9 us -> 39.8 us
  other arithmetic: 7.42 us -> 11.5 us
    all_gather x1, waiting for transfers between devices: 62.4 us -> 8.77 us  [on_device(): lax.all_gather(came_cot, 'tp', axis=2, tiled=True)]
    all_gather x1, waiting for transfers between devices: 10.2 us -> 62.4 us  [on_device(): lax.all_gather(came_rows, 'tp', axis=2, tiled=True)]
    all_gather x1 -> x0, waiting for transfers between devices: 27.7 us -> none  [on_device(): lax.all_gather(part_rows, 'grp', axis=0, tiled=True)]
    all_to_all x0 -> x1, blocking collectives: none -> 12 us  [on_device(): lax.all_to_all(jnp.stack([part_rows] * lax.axis_size('grp')), 'grp', 0, 0)]
    unnamed x7 -> x6, waiting for transfers between devices: 80.2 us -> 74.6 us
    all_to_all x1, blocking collectives: 17.2 us -> 12.2 us  [on_device(): lax.all_to_all(block_rows, 'tok', split_axis=0, concat_axis=0, tiled=True)]
    psum x1, blocking collectives: 32.2 us -> 27.4 us  [on_device(): doc_len = lax.psum(jnp.sum(doc_onehot, axis=0), ('tok', 'grp'))]
    another operation x2 -> x3, other arithmetic: 0.61 us -> 4.67 us  [the longest x1 4.05 us: on_device(): jnp.stack([part_rows] * lax.axis_size('grp'))]
  transfers between devices with their start and end apart: 7 -> 6, of which waited for: 7 -> 5; matrix products, arithmetic and copies ran while one was open for 15% -> 16% of each run, Pallas kernels for 0% -> 0%
where the time goes in v1:
time: 349 us
  waiting for transfers between devices  158 us (45%)
  blocking collectives  100 us (29%)
  matrix products  39.8 us (11%)
  local copies, waits for them, and re-layouts  18.1 us (5%)
  between operations  13.9 us (4%)
  other arithmetic  11.5 us (3%)
  starting transfers between devices  6.84 us (2%)
    unnamed x6, waiting for transfers between devices  74.6 us
    all_gather x1, waiting for transfers between devices, on_device(): lax.all_gather(came_rows, 'tp', axis=2, tiled=True)  62.4 us
    psum x1, blocking collectives, on_device(): squares = lax.psum(jnp.sum(wide_hidden * wide_hidden, axis=1), 'tp')  33.4 us
    psum x1, blocking collectives, on_device(): doc_len = lax.psum(jnp.sum(doc_onehot, axis=0), ('tok', 'grp'))  27.4 us
    unnamed x25, local copies, waits for them, and re-layouts  17.4 us
    all_to_all x1, blocking collectives, on_device(): lax.all_to_all(block_cot, 'tok', split_axis=0, concat_axis=0, tiled=True)  15.2 us
    all_to_all x1, blocking collectives, on_device(): lax.all_to_all(block_rows, 'tok', split_axis=0, concat_axis=0, tiled=True)  12.2 us
    all_to_all x1, blocking collectives, on_device(): lax.all_to_all(jnp.stack([part_rows] * lax.axis_size('grp')), 'grp', 0, 0)  12 us
  transfers between devices with their start and end apart: 6, of which 5 were waited for; matrix products, arithmetic and copies ran while one was open for 16% of the time, Pallas kernels for 0%

profile of v1, /device:TPU:1, one launch (start us, length us, event | category | flops | bytes accessed | tf_op | source)
XLA Modules:
  0.0 348.5 jit_solution(8825221306228375005)
XLA Ops:
  7.2 0.8 copy.31
  8.0 0.1 eq.56
  8.2 0.1 eq.52
  8.3 0.6 reduce-window.6
  8.9 0.2 slice_reduce_fusion
  9.1 0.1 fusion.27
  9.2 0.1 reshape.76
  9.4 0.1 copy.33
  9.5 0.7 multiply_add_fusion
  10.2 0.8 convert_reduce_fusion
  11.0 27.4 %psum.15 = f32[16]{0:T(128)S(1)} all-reduce(f32[16]{0:T(128)S(1)} %convert_reduce_fusion), channel_id=1, replica_groups=mesh['tok'=8,'tp'=16,'grp'=2] {'tok','grp'}, use_global_device_ids=true, to_apply=%region_10.11 | all-reduce | flops 16 | bytes 128 | tf_op jit(solution)/shard_map/psum | solution.py:44
  38.4 0.7 select_reduce_fusion.2
  39.1 0.7 broadcast_multiply_fusion
  39.8 1.5 select_reduce_fusion
  41.3 0.2 fusion.14
  41.5 15.2 %all_to_all.20 = bf16[8,40,384]{2,1,0:T(8,128)(2,1)} all-to-all(bf16[8,40,384]{2,1,0:T(8,128)(2,1)S(1)} %bitcast.63), channel_id=1, replica_groups=mesh['tok'=8,'tp'=16,'grp'=2] {'tok'}, dimensions={0} | all-to-all | bytes 491520 | tf_op jit(solution)/shard_map/all_to_all | solution.py:71
  56.7 0.0 all-gather.4.cloned.1.call-start
  56.8 0.7 convert_element_type.60
  57.5 1.0 fusion.19
  58.5 33.4 %psum.14 = f32[128]{0:T(128)S(1)} all-reduce(f32[128]{0:T(128)S(1)} %fusion.19), channel_id=1, replica_groups=mesh['tok'=8,'tp'=16,'grp'=2] {'tp'}, use_global_device_ids=true, to_apply=%region_6.7 | all-reduce | flops 128 | bytes 1024 | tf_op jit(solution)/shard_map/psum | solution.py:60
  91.9 1.2 convolution_convert_fusion.1
  93.1 12.2 %all_to_all.21 = bf16[8,40,384]{2,1,0:T(8,128)(2,1)} all-to-all(bf16[8,40,384]{2,1,0:T(8,128)(2,1)S(1)} %bitcast.62), channel_id=1, replica_groups=mesh['tok'=8,'tp'=16,'grp'=2] {'tok'}, dimensions={0} | all-to-all | bytes 491520 | tf_op jit(solution)/shard_map/all_to_all | solution.py:70
  105.3 0.0 all-gather.8.cloned.1.call-start
  105.4 8.8 %all-gather.6.cloned.1.call-done = bf16[8,40,6144]{2,1,0:T(8,128)(2,1)} async-done(((bf16[8,40,384]{2,1,0:T(8,128)(2,1)}), bf16[8,40,6144]{2,1,0:T(8,128)(2,1)}) %all-gather.6.cloned.1.call-update) | async-done | bytes 3932176 | tf_op jit(solution)/shard_map/all_gather | solution.py:75
  114.2 0.0 reduce-scatter.7.cloned.1.call-start
  114.2 62.4 %all-gather.4.cloned.1.call-done = bf16[8,40,6144]{2,1,0:T(8,128)(2,1)} async-done(((bf16[8,40,384]{2,1,0:T(8,128)(2,1)}), bf16[8,40,6144]{2,1,0:T(8,128)(2,1)}) %all-gather.4.cloned.1.call-update) | async-done | bytes 3932176 | tf_op jit(solution)/shard_map/all_gather | solution.py:74
  176.6 4.0 %pad_maximum_fusion = bf16[2,8,40,6144]{3,2,1,0:T(8,128)(2,1)S(1)} fusion(bf16[1,8,40,6144]{3,2,1,0:T(8,128)(2,1)} %bitcast.60), kind=kLoop, calls=%fused_computation.8 | loop fusion | flops 3932160 | bytes 11796480 | tf_op jit(solution)/shard_map/stack | solution.py:79
  180.6 12.0 %all_to_all.22 = bf16[2,8,40,6144]{3,2,1,0:T(8,128)(2,1)S(1)} all-to-all(bf16[2,8,40,6144]{3,2,1,0:T(8,128)(2,1)S(1)} %pad_maximum_fusion), channel_id=1, replica_groups=mesh['tok'=8,'tp'=16,'grp'=2] {'grp'}, dimensions={0} | all-to-all | bytes 15728640 | tf_op jit(solution)/shard_map/all_to_all | solution.py:79
  192.6 2.2 fusion.9
  194.8 2.1 copy-done.2
  196.9 0.5 copy-done.6
  197.4 3.0 multiply_convert_fusion.2
  200.5 0.7 copy-done.3
  201.2 5.4 %fusion = bf16[6144,640]{0,1:T(8,128)(2,1)} fusion(bf16[640,256]{1,0:T(8,128)(2,1)S(1)} %get-tuple-element.4, bf16[1,256,6144]{2,1,0:T(8,128)(2,1)S(1)} %copy-done.1), kind=kOutput, calls=%fused_computation.1 | convolution fusion | flops 2017198080 | bytes 11337728 | tf_op jit(solution)/shard_map/dot_general | solution.py:91
  206.6 10.4 %copy.34 = bf16[6144,640]{1,0:T(8,128)(2,1)} copy(bf16[6144,640]{0,1:T(8,128)(2,1)} %fusion) | data formatting | bytes 15728640
  217.1 0.2 reduce-scatter.5.cloned.1.call-start
  217.4 5.6 %fusion.4 = f32[640,256]{1,0:T(8,128)S(1)} fusion(bf16[640,6144]{1,0:T(8,128)(2,1)} %bitcast.54, bf16[1,256,6144]{2,1,0:T(8,128)(2,1)S(1)} %copy-done.1), kind=kOutput, calls=%fused_computation.9 | convolution fusion | flops 2013265920 | bytes 11665408 | tf_op jit(solution)/shard_map/dot_general | solution.py:13
  223.0 0.8 copy-done.9
  223.8 6.2 %fusion.11 = f32[256]{0:T(256)S(1)} fusion(bf16[1,6144,256]{2,1,0:T(8,128)(2,1)S(1)} %copy-done.5, bf16[640,6144]{1,0:T(8,128)(2,1)} %bitcast.58, f32[640,256]{1,0:T(8,128)S(1)} %copy-done.8, f32[640,256]{1,0:T(8,128)S(1)} %fusion.4, f32[640,256]{1,0:T(8,128)S(1)} %copy-done.10), kind=kOutput, calls=%fused_computation.16 | convolution fusion | flops 2021195520 | bytes 12977152 | tf_op jit(solution)/shard_map/dot_general | solution.py:20
  230.1 74.5 %reduce-scatter.7.cloned.1.call-done = bf16[384,640]{1,0:T(8,128)(2,1)} async-done(((bf16[6144,640]{1,0:T(8,128)(2,1)}), bf16[384,640]{1,0:T(8,128)(2,1)}) %reduce-scatter.7.cloned.1.call-update) | async-done | bytes 491536
  304.6 2.0 copy.35
  306.6 7.4 %fusion.12 = f32[256]{0:T(256)S(1)} fusion(bf16[1,6144,256]{2,1,0:T(8,128)(2,1)} %param.16, bf16[640,6144]{1,0:T(8,128)(2,1)} %bitcast.59, f32[640,256]{1,0:T(8,128)} %copy-done.9, f32[640,256]{1,0:T(8,128)} %copy-done.7), kind=kOutput, calls=%fused_computation.17 | convolution fusion | flops 2020540160 | bytes 12321792 | tf_op jit(solution)/shard_map/dot_general | solution.py:23
  314.0 7.7 %reduce-scatter.5.cloned.1.call-done = bf16[384,320]{0,1:T(8,128)(2,1)} async-done(((bf16[384,640]{0,1:T(8,128)(2,1)}), bf16[384,320]{0,1:T(8,128)(2,1)}) %reduce-scatter.5.cloned.1.call-update) | async-done | bytes 245776 | tf_op jit(solution)/shard_map/reduce_scatter | solution.py:98
  321.7 6.5 %all-to-all-start.2 = ((bf16[384,8,40]{0,2,1:T(8,128)(2,1)}), bf16[384,8,40]{0,2,1:T(8,128)(2,1)S(1)}, u32[]{:S(2)}, u32[]{:S(2)}) async-start(bf16[384,8,40]{0,2,1:T(8,128)(2,1)} %bitcast.64), calls=%async_computation.3 | async-start | bytes 491520 | tf_op jit(solution)/shard_map/all_to_all | solution.py:103
  328.1 6.5 %fusion.13 = f32[256]{0:T(256)S(1)} fusion(bf16[1,256,6144]{2,1,0:T(8,128)(2,1)S(1)} %copy-done.1, bf16[640,256]{1,0:T(8,128)(2,1)} %copy-done.3, bf16[640,6144]{1,0:T(8,128)(2,1)} %bitcast.55), kind=kOutput, calls=%fused_computation.18 | convolution fusion | flops 2019557120 | bytes 11338752 | tf_op jit(solution)/shard_map/dot_general | solution.py:26
  334.6 0.6 add_multiply_fusion
  335.2 4.7 %all-to-all-done.2 = bf16[384,8,40]{0,2,1:T(8,128)(2,1)S(1)} async-done(((bf16[384,8,40]{0,2,1:T(8,128)(2,1)}), bf16[384,8,40]{0,2,1:T(8,128)(2,1)S(1)}, u32[]{:S(2)}, u32[]{:S(2)}) %all-to-all-start.2) | async-done | bytes 245792 | tf_op jit(solution)/shard_map/all_to_all | solution.py:103
  339.9 2.0 fusion.15
  (31 shorter events, 0.3 us)
Async XLA Ops:
  7.2 34.2 %copy-start = (bf16[128,384]{1,0:T(8,128)(2,1)S(1)}, bf16[128,384]{1,0:T(8,128)(2,1)}, u32[]{:S(2)}) copy-start(bf16[128,384]{1,0:T(8,128)(2,1)} %param.14) | copy-start | bytes 294916
  7.2 107.0 %all-gather.6.cloned.1.call-start = ((), (), s32[]{:S(2)}) async-start(), calls=%async_computation.8 | async-start | bytes 4177920 | tf_op jit(solution)/shard_map/all_gather | solution.py:75
  56.7 119.9 %all-gather.4.cloned.1.call-start = ((), (), s32[]{:S(2)}) async-start(), calls=%async_computation.6 | async-start | bytes 4177920 | tf_op jit(solution)/shard_map/all_gather | solution.py:74
  105.3 112.0 %all-gather.8.cloned.1.call-start = ((), (), s32[]{:S(2)}) async-start(), calls=%async_computation.9 | async-start | bytes 11796480 | tf_op jit(solution)/shard_map/all_gather | solution.py:81
  114.2 190.4 %reduce-scatter.7.cloned.1.call-start = ((), (), s32[]{:S(2)}) async-start(), calls=%async_computation.10 | async-start | bytes 8355840
  180.6 12.0 %copy-start.4 = (bf16[1,6144,256]{2,1,0:T(8,128)(2,1)S(1)}, bf16[1,6144,256]{2,1,0:T(8,128)(2,1)}, u32[]{:S(2)}) copy-start(bf16[1,6144,256]{2,1,0:T(8,128)(2,1)} %param.15) | copy-start | bytes 9437188
  192.6 4.3 %copy-start.2 = (bf16[2,8,40,6144]{3,2,1,0:T(8,128)(2,1)}, bf16[2,8,40,6144]{3,2,1,0:T(8,128)(2,1)S(1)}, u32[]{:S(2)}) copy-start(bf16[2,8,40,6144]{3,2,1,0:T(8,128)(2,1)S(1)} %all_to_all.22) | copy-start | bytes 23592964
  192.6 4.8 %copy-start.6 = (bf16[1,6144,256]{2,1,0:T(8,128)(2,1)S(1)}, bf16[1,6144,256]{2,1,0:T(8,128)(2,1)}, u32[]{:S(2)}) copy-start(bf16[1,6144,256]{2,1,0:T(8,128)(2,1)} %param.16) | copy-start | bytes 9437188
  197.4 3.0 copy-start.7
  197.4 3.8 %copy-start.1 = (bf16[1,256,6144]{2,1,0:T(8,128)(2,1)S(1)}, bf16[1,256,6144]{2,1,0:T(8,128)(2,1)}, u32[]{:S(2)}) copy-start(bf16[1,256,6144]{2,1,0:T(8,128)(2,1)} %param.17) | copy-start | bytes 9437188
  200.5 0.7 copy-start.3
  217.1 104.6 %reduce-scatter.5.cloned.1.call-start = ((), (), s32[]{:S(2)}) async-start(), calls=%async_computation.7 | async-start | bytes 737280 | tf_op jit(solution)/shard_map/reduce_scatter | solution.py:98
  217.3 6.5 %copy-start.5 = (bf16[1,6144,256]{2,1,0:T(8,128)(2,1)S(1)}, bf16[1,6144,256]{2,1,0:T(8,128)(2,1)}, u32[]{:S(2)}) copy-start(bf16[1,6144,256]{2,1,0:T(8,128)(2,1)} %param.15) | copy-start | bytes 9437188
  217.4 6.5 %copy-start.8 = (f32[640,256]{1,0:T(8,128)S(1)}, f32[640,256]{1,0:T(8,128)}, u32[]{:S(2)}) copy-start(f32[640,256]{1,0:T(8,128)} %copy-done.7) | copy-start | bytes 1966084
  217.4 6.5 %copy-start.10 = (f32[640,256]{1,0:T(8,128)S(1)}, f32[640,256]{1,0:T(8,128)}, u32[]{:S(2)}) copy-start(f32[640,256]{1,0:T(8,128)} %get-tuple-element.5) | copy-start | bytes 1966084
  223.0 0.8 copy-start.9
  321.7 18.3 %all-to-all-start.2 = ((bf16[384,8,40]{0,2,1:T(8,128)(2,1)}), bf16[384,8,40]{0,2,1:T(8,128)(2,1)S(1)}, u32[]{:S(2)}, u32[]{:S(2)}) async-start(bf16[384,8,40]{0,2,1:T(8,128)(2,1)} %bitcast.64), calls=%async_computation.3 | async-start | bytes 491520 | tf_op jit(solution)/shard_map/all_to_all | solution.py:103
Sparse Core Ops, SparseCore 0:
  56.9 57.2 all-gather.5
  116.5 59.9 all-gather.3
  178.4 25.9 all-gather.7
  217.2 87.2 reduce-scatter.6
  306.9 14.6 reduce-scatter.4
